TPU v7x, 256 devices: a whole 4x4x8 slice. The times are simulated.
256 devices in a mesh: freq: 8 (over z_lo, core), col: 32 (over x, y, z_hi).
Axes of the slice: x: 4, y: 4, z: 8 (z_hi: 2, z_lo: 4; z = z_hi * 4 + z_lo), core: 2. Of those that a mesh axis runs over, the one named last changes fastest.
Arguments:
- spectra: bfloat16 [2, 16, 4096, 4096], P(None, None, 'freq', 'col'), may hold values from -0.62890625 to 0.62890625
- wavelet: float32 [2, 16], P(None, 'freq'), may hold values from -1.5 to 1.5
Outputs:
- predicted: bfloat16 [2, 16, 384, 4096], P(None, 'freq', None, 'col')
All inputs are finite; a program needn't handle non-finite values.
Results may differ from a plain program's by a relative error of at most 0.001.
Values may be sent and summed in bfloat16 or wider, within the bound.
No kernel may reach another device: no remote copies, remote signals or barrier semaphores. Data moves between devices by JAX's collectives and lax.ppermute only.
A program may use at most 128 MiB of HBM per device.

v0:
```python
import jax
import jax.numpy as jnp
from jax import lax
from jax.sharding import PartitionSpec as P

NOUT = 384


def complex_product(left, right, form):
    real_part = jnp.einsum(
        form, left[0], right[0], preferred_element_type=jnp.float32
    ) - jnp.einsum(form, left[1], right[1], preferred_element_type=jnp.float32)
    imag_part = jnp.einsum(
        form, left[0], right[1], preferred_element_type=jnp.float32
    ) + jnp.einsum(form, left[1], right[0], preferred_element_type=jnp.float32)
    return jnp.stack([real_part, imag_part])


def predict(slab, window):
    upper = slab[:, :, :window, :]
    return complex_product(lax.all_gather(upper, "col", axis=3, tiled=True), slab, "fnw,fwc->fnc")


def local(spectra, wavelet):
    window = NOUT
    slab = lax.all_to_all(spectra, "freq", split_axis=1, concat_axis=2, tiled=True)
    product = predict(slab, window)
    wave_real = wavelet[0][:, None, None]
    wave_imag = wavelet[1][:, None, None]
    real_out = -(wave_real * product[0] - wave_imag * product[1])
    imag_out = -(wave_real * product[1] + wave_imag * product[0])
    return jnp.stack([real_out, imag_out]).astype(jnp.bfloat16)


def solution(mesh):
    return jax.shard_map(
        local,
        mesh=mesh,
        in_specs=(P(None, None, "freq", "col"), P(None, "freq")),
        out_specs=P(None, "freq", None, "col"),
        check_vma=False,
    )
```

profile of v0, /device:TPU:8, one launch (start us, length us, event | category | flops | bytes accessed | tf_op | source)
XLA Modules:
  0.0 411.4 jit_solution(6084486596494399329)
XLA Ops:
  6.5 0.0 all-gather.2.cloned.1.call-start
  6.5 2.5 copy.4
  9.0 99.7 %all_to_all.18 = bf16[2,16,512,128]{3,2,0,1:T(8,128)(2,1)S(1)} all-to-all(bf16[2,16,512,128]{3,2,0,1:T(8,128)(2,1)S(1)} %copy.4), channel_id=1, replica_groups=mesh['freq'=8,'col'=32] {'freq'}, dimensions={1} | all-to-all | bytes 8388608 | tf_op jit(solution)/shard_map/all_to_all | solution.py:26
  108.7 0.0 copy-start.2
  108.7 0.4 copy.8
  109.1 0.0 copy-start
  109.1 1.9 copy-done
  111.1 0.8 slice.34
  111.8 0.0 all-gather.2.cloned.1.call-update
  111.9 0.0 copy-done.2
  111.9 3.9 fusion.8
  115.8 274.3 %all-gather.2.cloned.1.call-done = bf16[2,2,384,4096]{3,2,1,0:T(8,128)(2,1)} async-done(((bf16[2,2,384,128]{3,2,1,0:T(8,128)(2,1)}), bf16[2,2,384,4096]{3,2,1,0:T(8,128)(2,1)}) %all-gather.2.cloned.1.call-update) | async-done | bytes 12582928 | tf_op jit(solution)/shard_map/all_gather | solution.py:21
  390.1 0.0 copy-start.1
  390.1 0.0 copy-start.3
  390.1 4.7 %fusion.1 = f32[2,384,128]{2,1,0:T(8,128)S(1)} fusion(bf16[2,4096,128]{2,1,0:T(8,128)(2,1)S(1)} %bitcast.36, bf16[2,2,384,4096]{3,2,1,0:T(8,128)(2,1)} %all-gather.2.cloned.1.call-done), kind=kOutput, calls=%fused_computation.3 | convolution fusion | flops 805306368 | bytes 8781824 | tf_op jit(solution)/shard_map/fnw,fwc->fnc/dot_general | solution.py:10
  394.8 0.0 copy-done.1
  394.8 5.3 %fusion = f32[2,384,128]{2,1,0:T(8,128)S(1)} fusion(bf16[2,4096,128]{2,1,0:T(8,128)(2,1)S(1)} %bitcast.38, bf16[2,2,384,4096]{3,2,1,0:T(8,128)(2,1)} %all-gather.2.cloned.1.call-done), kind=kOutput, calls=%fused_computation.2 | convolution fusion | flops 805306368 | bytes 8781824 | tf_op jit(solution)/shard_map/fnw,fwc->fnc/dot_general | solution.py:13
  400.1 0.0 copy-done.3
  400.1 1.8 fusion.4
  401.9 1.8 fusion.6
  403.8 0.8 pad_maximum_fusion
  (1 shorter events, 0.0 us)
Async XLA Ops:
  6.5 383.5 %all-gather.2.cloned.1.call-start = ((), (), s32[]{:S(2)}) async-start(), calls=%async_computation.1 | async-start | bytes 12976128 | tf_op jit(solution)/shard_map/all_gather | solution.py:21
  108.7 3.2 copy-start.2
  109.1 1.9 copy-start
  390.1 4.7 %copy-start.1 = (bf16[1,2,8,512,128]{4,3,2,1,0:T(8,128)(2,1)S(1)}, bf16[1,2,8,512,128]{4,3,2,1,0:T(8,128)(2,1)}, u32[]{:S(2)}) copy-start(bf16[1,2,8,512,128]{4,3,2,1,0:T(8,128)(2,1)} %get-tuple-element.5) | copy-start | bytes 6291460
  390.1 10.1 %copy-start.3 = (bf16[2,2,384,4096]{3,2,1,0:T(8,128)(2,1)S(1)}, bf16[2,2,384,4096]{3,2,1,0:T(8,128)(2,1)}, u32[]{:S(2)}) copy-start(bf16[2,2,384,4096]{3,2,1,0:T(8,128)(2,1)} %all-gather.2.cloned.1.call-done) | copy-start | bytes 37748740
Sparse Core Ops, SparseCore 0:
  112.0 278.0 all-gather.1
where the time goes:
time: 412 us; the launch traced here: 411 us
  waiting for transfers between devices  274 us (67%)
  blocking collectives  99.7 us (24%)
  matrix products  13.6 us (3%)
  between operations  13.5 us (3%)
  local copies, waits for them, and re-layouts  9.51 us (2%)
    all_gather x1, waiting for transfers between devices, predict(): lax.all_gather(upper, 'col', axis=3, tiled=True)  274 us
    all_to_all x1, blocking collectives, local(): lax.all_to_all(spectra, 'freq', split_axis=1, concat_axis=2, tiled=True)  99.7 us
  transfers between devices with their start and end apart: 1, of which 1 were waited for; matrix products, arithmetic and copies ran while one was open for 1% of the time, Pallas kernels for 0%

commit v1 on v0

--- a/solution.py
+++ b/solution.py
@@ -18,7 +18,13 @@
 
 def predict(slab, window):
     upper = slab[:, :, :window, :]
-    return complex_product(lax.all_gather(upper, "col", axis=3, tiled=True), slab, "fnw,fwc->fnc")
+    return complex_product(
+        jnp.concatenate(
+            lax.all_to_all(jnp.stack([upper] * lax.axis_size("col")), "col", 0, 0), axis=3
+        ),
+        slab,
+        "fnw,fwc->fnc",
+    )
 
 
 def local(spectra, wavelet):

time: 412 us -> 514 us (1.25)
  the two profiles are of different devices: /device:TPU:8 before, /device:TPU:128 now
where the time goes in v1:
time: 514 us
  waiting for transfers between devices  330 us (64%)
  blocking collectives  97 us (19%)
  local copies, waits for them, and re-layouts  63.6 us (12%)
  starting transfers between devices  12.6 us (2%)
  matrix products  10.1 us (2%)
    all_to_all x1, waiting for transfers between devices, predict(): lax.all_to_all(jnp.stack([upper] * lax.axis_size('col')), 'col', 0, 0)  330 us
    all_to_all x1, blocking collectives, local(): lax.all_to_all(spectra, 'freq', split_axis=1, concat_axis=2, tiled=True)  97 us
    slice x2, local copies, waits for them, and re-layouts, complex_product(): left[1]  19.1 us
    all_to_all x1, starting transfers between devices, predict(): lax.all_to_all(jnp.stack([upper] * lax.axis_size('col')), 'col', 0, 0)  12.6 us
    squeeze x1, local copies, waits for them, and re-layouts, complex_product(): left[1]  10.3 us
    squeeze x1, local copies, waits for them, and re-layouts, complex_product(): left[0]  10.3 us
  transfers between devices with their start and end apart: 1, of which 1 were waited for; matrix products, arithmetic and copies ran while one was open for 1% of the time, Pallas kernels for 0%

profile of v1, /device:TPU:128, one launch (start us, length us, event | category | flops | bytes accessed | tf_op | source)
XLA Modules:
  0.0 513.7 jit_solution(15956375739502170500)
XLA Ops:
  0.0 2.5 copy.4
  2.5 97.0 %all_to_all.23 = bf16[2,16,512,128]{3,2,0,1:T(8,128)(2,1)S(1)} all-to-all(bf16[2,16,512,128]{3,2,0,1:T(8,128)(2,1)S(1)} %copy.4), channel_id=1, replica_groups=mesh['freq'=8,'col'=32] {'freq'}, dimensions={1} | all-to-all | bytes 8388608 | tf_op jit(solution)/shard_map/all_to_all | solution.py:32
  99.5 0.4 copy.10
  99.9 0.0 copy-start.2
  99.9 2.0 copy-done.2
  101.9 7.6 %stack.11 = bf16[32,2,2,384,128]{4,3,2,1,0:T(8,128)(2,1)} broadcast(bf16[2,2,384,128]{3,2,1,0:T(8,128)(2,1)S(1)} %slice.36), dimensions={1,2,3,4} | broadcast | bytes 12976128 | tf_op jit(solution)/shard_map/stack | solution.py:23
  109.5 12.6 %all-to-all-start.1 = ((bf16[32,2,2,384,128]{4,3,2,1,0:T(8,128)(2,1)}), bf16[32,2,2,384,128]{4,3,2,1,0:T(8,128)(2,1)}, u32[]{:S(2)}, u32[]{:S(2)}) async-start(bf16[32,2,2,384,128]{4,3,2,1,0:T(8,128)(2,1)} %stack.11), calls=%async_computation.1 | async-start | bytes 25165824 | tf_op jit(solution)/shard_map/all_to_all | solution.py:23
  122.2 0.0 copy-done.3
  122.2 3.9 fusion.3
  126.1 329.6 %all-to-all-done.1 = bf16[32,2,2,384,128]{4,3,2,1,0:T(8,128)(2,1)} async-done(((bf16[32,2,2,384,128]{4,3,2,1,0:T(8,128)(2,1)}), bf16[32,2,2,384,128]{4,3,2,1,0:T(8,128)(2,1)}, u32[]{:S(2)}, u32[]{:S(2)}) %all-to-all-start.1) | async-done | bytes 12582944 | tf_op jit(solution)/shard_map/all_to_all | solution.py:23
  455.7 9.6 %fusion.2 = (bf16[1,2,384,32,128]{4,2,1,0,3:T(8,128)(2,1)}, bf16[1,2,384,32,128]{4,2,1,0,3:T(8,128)(2,1)S(1)}) fusion(bf16[2,2,384,32,128]{4,2,1,0,3:T(8,128)(2,1)} %bitcast.4), kind=kLoop, calls=%fused_computation.10 | loop fusion | bytes 25165824 | tf_op jit(solution)/shard_map/slice | solution.py:12
  465.3 6.7 %copy.6 = bf16[1,2,384,32,128]{4,3,2,1,0:T(8,128)(2,1)} copy(bf16[1,2,384,32,128]{4,2,1,0,3:T(8,128)(2,1)S(1)} %get-tuple-element.6) | data formatting | bytes 12582912 | tf_op jit(solution)/shard_map/slice | solution.py:11
  472.0 10.3 %squeeze.16 = bf16[2,384,4096]{2,1,0:T(8,128)(2,1)} reshape(bf16[1,2,384,32,128]{4,3,2,1,0:T(8,128)(2,1)} %copy.6) | data formatting | bytes 12582912 | tf_op jit(solution)/shard_map/squeeze | solution.py:11
  482.3 9.4 %copy.7 = bf16[1,2,384,32,128]{4,3,2,1,0:T(8,128)(2,1)} copy(bf16[1,2,384,32,128]{4,2,1,0,3:T(8,128)(2,1)} %get-tuple-element.5) | data formatting | bytes 12582912 | tf_op jit(solution)/shard_map/slice | solution.py:12
  491.8 10.3 %squeeze.18 = bf16[2,384,4096]{2,1,0:T(8,128)(2,1)} reshape(bf16[1,2,384,32,128]{4,3,2,1,0:T(8,128)(2,1)} %copy.7) | data formatting | bytes 12582912 | tf_op jit(solution)/shard_map/squeeze | solution.py:12
  502.1 4.7 fusion.5
  506.8 0.0 slice-start.1
  506.8 0.0 copy-done
  506.8 0.5 copy-done.1
  507.3 1.8 fusion.4
  509.1 0.2 slice-done.1
  509.3 1.8 convolution_add_fusion
  511.1 1.8 fusion
  513.0 0.8 pad_maximum_fusion
  (8 shorter events, 0.0 us)
Async XLA Ops:
  99.9 2.0 copy-start.2
  109.5 12.7 %copy-start.3 = (f32[2,2]{1,0:T(2,128)S(1)}, f32[2,2]{1,0:T(2,128)}, u32[]{:S(2)}) copy-start(f32[2,2]{1,0:T(2,128)} %param.3) | copy-start | bytes 52
  109.5 346.2 %all-to-all-start.1 = ((bf16[32,2,2,384,128]{4,3,2,1,0:T(8,128)(2,1)}), bf16[32,2,2,384,128]{4,3,2,1,0:T(8,128)(2,1)}, u32[]{:S(2)}, u32[]{:S(2)}) async-start(bf16[32,2,2,384,128]{4,3,2,1,0:T(8,128)(2,1)} %stack.11), calls=%async_computation.1 | async-start | bytes 25165824 | tf_op jit(solution)/shard_map/all_to_all | solution.py:23
  502.1 4.7 copy-start
  502.1 5.2 %copy-start.1 = (bf16[1,2,8,512,128]{4,3,2,1,0:T(8,128)(2,1)S(1)}, bf16[1,2,8,512,128]{4,3,2,1,0:T(8,128)(2,1)}, u32[]{:S(2)}) copy-start(bf16[1,2,8,512,128]{4,3,2,1,0:T(8,128)(2,1)} %get-tuple-element.8) | copy-start | bytes 6291460
  502.1 7.0 %slice-start = ((s8[6291456]{0:T(1024)(128)(4,1)}), s8[4194304]{0:T(1024)(128)(4,1)S(1)}, s32[]{:S(2)}) async-start(s8[6291456]{0:T(1024)(128)(4,1)} %bitcast.29), calls=%async_computation.2 | async-start | bytes 8388608
  506.8 2.5 slice-start.1
